TPU v7x, 32 devices: a whole 2x2x4 slice. The times are simulated.
32 devices in a mesh: dp: 4 (over y, x), row: 4 (over z), col: 2 (over core).
Axes of the slice: x: 2, y: 2, z: 4, core: 2. Of those that a mesh axis runs over, the one named last changes fastest.
Arguments:
- patches: bfloat16 [4, 2, 1408, 768], P('dp', None, ('row', 'col')), may hold values from -6 to 6
- picture_ids: int32 [4, 2, 1408], P('dp'), may hold values from 0 to 3, never falling along the last dimension, each value on 1 to 1024 neighbouring positions
- ln1_gain: float32 [768], replicated, may hold values from 0.5 to 1.5
- ln1_bias: float32 [768], replicated, may hold values from -3 to 3
- w_query: bfloat16 [768, 768], P(('dp', 'row'), 'col'), may hold values from -0.21875 to 0.21875
- w_key: bfloat16 [768, 768], P(('dp', 'row'), 'col'), may hold values from -0.21875 to 0.21875
- w_value: bfloat16 [768, 768], P(('dp', 'row'), 'col'), may hold values from -0.21875 to 0.21875
- q_gain: float32 [64], replicated, may hold values from 0.1 to 1.9
- k_gain: float32 [64], replicated, may hold values from 0.1 to 1.9
- w_out: bfloat16 [768, 768], P('col', ('dp', 'row')), may hold values from -2 to 2
- ln2_gain: float32 [768], replicated, may hold values from 0.5 to 1.5
- ln2_bias: float32 [768], replicated, may hold values from -3 to 3
- w_up: bfloat16 [768, 3072], P(('dp', 'row'), 'col'), may hold values from -0.21875 to 0.21875
- w_down: bfloat16 [3072, 768], P('col', ('dp', 'row')), may hold values from -0.109375 to 0.109375
- cotangent: bfloat16 [4, 2, 1408, 768], P('dp', None, ('row', 'col')), may hold values from -6 to 6
Outputs:
- result: bfloat16 [4, 2, 1408, 768], P('dp', None, ('row', 'col'))
- grad_input: float32 [4, 2, 1408, 768], P('dp', None, ('row', 'col'))
- grad_ln1_gain: float32 [768], replicated
- grad_ln1_bias: float32 [768], replicated
- grad_w_query: float32 [768, 768], P(('dp', 'row'), 'col')
- grad_w_key: float32 [768, 768], P(('dp', 'row'), 'col')
- grad_w_value: float32 [768, 768], P(('dp', 'row'), 'col')
- grad_q_gain: float32 [64], replicated
- grad_k_gain: float32 [64], replicated
- grad_w_out: float32 [768, 768], P('col', ('dp', 'row'))
- grad_ln2_gain: float32 [768], replicated
- grad_ln2_bias: float32 [768], replicated
- grad_w_up: float32 [768, 3072], P(('dp', 'row'), 'col')
- grad_w_down: float32 [3072, 768], P('col', ('dp', 'row'))
Inputs may be any that keep to these rules, and one draw needn't show every extreme that they name: `picture_ids`: in each packed row the picture ids never fall, every id is used, each picture covers 1 to 1024 patches and one covers exactly 1024.
All inputs are finite; a program needn't handle non-finite values.
Results may differ from a plain program's by a relative error of at most 0.017.
Values may be sent and summed in bfloat16 or wider, within the bound.
No kernel may reach another device: no remote copies, remote signals or barrier semaphores. Data moves between devices by JAX's collectives and lax.ppermute only.
A program may use at most 128 MiB of HBM per device.

v0:
```python
import jax
import jax.numpy as jnp
from jax import lax
from jax.sharding import PartitionSpec as P

HD = 64


EPSILON = 1e-06
MASKED_SCORE = -1e30


def contract(left_arr, right_arr, left_dim, right_dim):
    return lax.dot_general(
        left_arr,
        right_arr,
        (((left_dim,), (right_dim,)), ((), ())),
        preferred_element_type=jnp.float32,
    )


def layer_norm(tensor, gain_vec, bias_vec):
    average = jnp.mean(tensor, axis=-1, keepdims=True)
    centred = tensor - average
    variance = jnp.mean(centred * centred, axis=-1, keepdims=True)
    return centred * lax.rsqrt(variance + EPSILON) * gain_vec + bias_vec


def gelu_tanh(tensor):
    return jax.nn.gelu(tensor, approximate=True)


def fetch(blocks):
    return (
        lax.all_gather(blocks[0], ("dp", "row"), axis=0, tiled=True),
        lax.all_gather(blocks[1], ("dp", "row"), axis=0, tiled=True),
        lax.all_gather(blocks[2], ("dp", "row"), axis=0, tiled=True),
        lax.all_gather(blocks[3], ("dp", "row"), axis=0, tiled=True),
        lax.all_gather(blocks[4], ("dp", "row"), axis=1, tiled=True),
        lax.all_gather(blocks[5], ("dp", "row"), axis=1, tiled=True),
    )


def spread(tensor):
    return lax.all_gather(tensor, "col", axis=0, tiled=True)


def collect(tensor):
    return lax.psum_scatter(
        tensor.astype(jnp.bfloat16), "col", scatter_dimension=0, tiled=True
    ).astype(jnp.float32)


def reduce_grads(weight_part, gain_part):
    shards = (
        lax.psum_scatter(weight_part[0], ("dp", "row"), scatter_dimension=0, tiled=True),
        lax.psum_scatter(weight_part[1], ("dp", "row"), scatter_dimension=0, tiled=True),
        lax.psum_scatter(weight_part[2], ("dp", "row"), scatter_dimension=0, tiled=True),
        lax.psum_scatter(weight_part[3], ("dp", "row"), scatter_dimension=0, tiled=True),
        lax.psum_scatter(weight_part[4], ("dp", "row"), scatter_dimension=1, tiled=True),
        lax.psum_scatter(weight_part[5], ("dp", "row"), scatter_dimension=1, tiled=True),
    )
    summed = lax.psum(gain_part, ("dp", "row", "col"))
    return (shards, summed)


def masked_scores(queries_low, keys_all, same_pic):
    scores = jnp.einsum("qhd,khd->hqk", queries_low, keys_all, preferred_element_type=jnp.float32)
    return jnp.where(same_pic[None], scores, MASKED_SCORE)


def micro_layer(patch_part, id_row, cot_part, whole, smalls):
    w_q, w_k, w_v, w_u, w_o, w_d = whole
    gain_one, bias_one, gain_query, gain_key, gain_two, bias_two = smalls
    row_tokens = patch_part.shape[0] * lax.axis_size("col")
    heads_loc = w_q.shape[1] // HD
    factor = float(HD) ** (-0.5)
    query_ids = lax.dynamic_slice_in_dim(id_row, lax.axis_index("row") * row_tokens, row_tokens)
    same_pic = query_ids[:, None] == id_row[None, :]
    patch_f = patch_part.astype(jnp.float32)
    normed, ln1_pull = jax.vjp(layer_norm, patch_f, gain_one, bias_one)
    normed_all = spread(normed.astype(jnp.bfloat16))
    queries_raw = jnp.dot(normed_all, w_q, preferred_element_type=jnp.float32).reshape(
        row_tokens, heads_loc, HD
    )
    keys_raw = jnp.dot(normed_all, w_k, preferred_element_type=jnp.float32).reshape(
        row_tokens, heads_loc, HD
    )
    values_raw = jnp.dot(normed_all, w_v, preferred_element_type=jnp.float32)

    def query_norm(tensor, gain_vec):
        return layer_norm(tensor, gain_vec, 0.0) * factor

    def key_norm(tensor, gain_vec):
        return layer_norm(tensor, gain_vec, 0.0)

    queries_n, query_pull = jax.vjp(query_norm, queries_raw, gain_query)
    keys_n, key_pull = jax.vjp(key_norm, keys_raw, gain_key)
    queries_low = queries_n.astype(jnp.bfloat16)
    keys_low = keys_n.astype(jnp.bfloat16).reshape(row_tokens, heads_loc * HD)
    values_low = values_raw.astype(jnp.bfloat16)
    keys_all, values_all = (
        lax.all_gather(keys_low, "row", axis=0, tiled=True),
        lax.all_gather(values_low, "row", axis=0, tiled=True),
    )
    seq_len = keys_all.shape[0]
    keys_all = keys_all.reshape(seq_len, heads_loc, HD)
    values_all = values_all.reshape(seq_len, heads_loc, HD)
    masked = masked_scores(queries_low, keys_all, same_pic)
    row_max = jnp.max(masked, axis=-1, keepdims=True)
    expo_vals = jnp.exp(masked - row_max)
    row_total = jnp.sum(expo_vals, axis=-1, keepdims=True)
    prob_full = expo_vals / row_total
    probs_low = prob_full.astype(jnp.bfloat16)
    attended = jnp.einsum("hqk,khd->qhd", probs_low, values_all, preferred_element_type=jnp.float32)
    attended_low = attended.reshape(row_tokens, heads_loc * HD).astype(jnp.bfloat16)
    mixed = patch_f + collect(jnp.dot(attended_low, w_o, preferred_element_type=jnp.float32))
    normed_two, ln2_pull = jax.vjp(layer_norm, mixed, gain_two, bias_two)
    normed_two_all = spread(normed_two.astype(jnp.bfloat16))
    up_proj = jnp.dot(normed_two_all, w_u, preferred_element_type=jnp.float32)
    activated, gelu_pull = jax.vjp(gelu_tanh, up_proj)
    activated_low = activated.astype(jnp.bfloat16)
    result = mixed + collect(jnp.dot(activated_low, w_d, preferred_element_type=jnp.float32))
    branch_grad = spread(cot_part)
    d_act = contract(branch_grad, w_d, 1, 1)
    (d_up,) = gelu_pull(d_act)
    d_up_low = d_up.astype(jnp.bfloat16)
    grad_wd = contract(activated_low, branch_grad, 0, 0)
    grad_wu = contract(normed_two_all, d_up_low, 0, 0)
    d_normed_two = collect(contract(d_up_low, w_u, 1, 1))
    d_mixed, grad_g2, grad_b2 = ln2_pull(d_normed_two)
    d_mixed = d_mixed + cot_part.astype(jnp.float32)
    d_branch = spread(d_mixed.astype(jnp.bfloat16))
    grad_wo = contract(attended_low, d_branch, 0, 0)
    d_attended = (
        contract(d_branch, w_o, 1, 1).astype(jnp.bfloat16).reshape(row_tokens, heads_loc, HD)
    )
    masked_again = masked_scores(queries_low, keys_all, same_pic)
    prob_again = jnp.exp(masked_again - row_max) / row_total
    d_probs = jnp.einsum("qhd,khd->hqk", d_attended, values_all, preferred_element_type=jnp.float32)
    inner_sum = jnp.sum(prob_again * d_probs, axis=-1, keepdims=True)
    d_scores = (prob_again * (d_probs - inner_sum)).astype(jnp.bfloat16)
    d_queries_low = jnp.einsum(
        "hqk,khd->qhd", d_scores, keys_all, preferred_element_type=jnp.float32
    )
    probs_low_again = prob_again.astype(jnp.bfloat16)
    d_keys_part = jnp.einsum(
        "hqk,qhd->khd", d_scores, queries_low, preferred_element_type=jnp.float32
    ).reshape(seq_len, heads_loc * HD)
    d_values_part = jnp.einsum(
        "hqk,qhd->khd", probs_low_again, d_attended, preferred_element_type=jnp.float32
    ).reshape(seq_len, heads_loc * HD)
    d_keys_low, d_values_raw = (
        lax.psum_scatter(
            d_keys_part.astype(jnp.bfloat16), "row", scatter_dimension=0, tiled=True
        ).astype(jnp.float32),
        lax.psum_scatter(
            d_values_part.astype(jnp.bfloat16), "row", scatter_dimension=0, tiled=True
        ).astype(jnp.float32),
    )
    d_queries, grad_gq = query_pull(d_queries_low)
    d_keys, grad_gk = key_pull(d_keys_low.reshape(row_tokens, heads_loc, HD))
    dq_low = d_queries.reshape(row_tokens, heads_loc * HD).astype(jnp.bfloat16)
    dk_low = d_keys.reshape(row_tokens, heads_loc * HD).astype(jnp.bfloat16)
    dv_low = d_values_raw.astype(jnp.bfloat16)
    grad_wq = contract(normed_all, dq_low, 0, 0)
    grad_wk = contract(normed_all, dk_low, 0, 0)
    grad_wv = contract(normed_all, dv_low, 0, 0)
    d_normed_part = (
        contract(dq_low, w_q, 1, 1) + contract(dk_low, w_k, 1, 1) + contract(dv_low, w_v, 1, 1)
    )
    d_normed = collect(d_normed_part)
    d_first, grad_g1, grad_b1 = ln1_pull(d_normed)
    grad_in = d_mixed + d_first
    weight_part = (grad_wq, grad_wk, grad_wv, grad_wu, grad_wo, grad_wd)
    gain_part = (grad_g1, grad_b1, grad_gq, grad_gk, grad_g2, grad_b2)
    return (result.astype(jnp.bfloat16), grad_in, weight_part, gain_part)


def per_device(
    patches,
    picture_ids,
    ln1_gain,
    ln1_bias,
    w_query,
    w_key,
    w_value,
    q_gain,
    k_gain,
    w_out,
    ln2_gain,
    ln2_bias,
    w_up,
    w_down,
    cotangent,
):
    blocks = (w_query, w_key, w_value, w_up, w_out, w_down)
    smalls = (ln1_gain, ln1_bias, q_gain, k_gain, ln2_gain, ln2_bias)
    weight_zero = tuple((jnp.zeros(block.shape, jnp.float32) for block in blocks))
    gain_zero = tuple((jnp.zeros(small_arr.shape, jnp.float32) for small_arr in smalls))

    def step(carry, scan_items):
        weight_sum, gain_sum = carry
        patch_part, id_row, cot_part = scan_items
        whole = fetch(blocks)
        result, grad_in, weight_part, gain_part = micro_layer(
            patch_part, id_row, cot_part, whole, smalls
        )
        weight_part, gain_part = reduce_grads(weight_part, gain_part)
        weight_sum = tuple((acc + piece for acc, piece in zip(weight_sum, weight_part)))
        gain_sum = tuple((acc + piece for acc, piece in zip(gain_sum, gain_part)))
        return ((weight_sum, gain_sum), (result, grad_in))

    (weight_sum, gain_sum), (results, grads_in) = lax.scan(
        step, (weight_zero, gain_zero), (patches[0], picture_ids[0], cotangent[0])
    )
    grad_wq, grad_wk, grad_wv, grad_wu, grad_wo, grad_wd = weight_sum
    grad_g1, grad_b1, grad_gq, grad_gk, grad_g2, grad_b2 = gain_sum
    return (
        results[None],
        grads_in[None],
        grad_g1,
        grad_b1,
        grad_wq,
        grad_wk,
        grad_wv,
        grad_gq,
        grad_gk,
        grad_wo,
        grad_g2,
        grad_b2,
        grad_wu,
        grad_wd,
    )


def solution(mesh):
    return jax.shard_map(
        per_device,
        mesh=mesh,
        in_specs=(
            P("dp", None, ("row", "col"), None),
            P("dp", None, None),
            P(),
            P(),
            P(("dp", "row"), "col"),
            P(("dp", "row"), "col"),
            P(("dp", "row"), "col"),
            P(),
            P(),
            P("col", ("dp", "row")),
            P(),
            P(),
            P(("dp", "row"), "col"),
            P("col", ("dp", "row")),
            P("dp", None, ("row", "col"), None),
        ),
        out_specs=(
            P("dp", None, ("row", "col"), None),
            P("dp", None, ("row", "col"), None),
            P(),
            P(),
            P(("dp", "row"), "col"),
            P(("dp", "row"), "col"),
            P(("dp", "row"), "col"),
            P(),
            P(),
            P("col", ("dp", "row")),
            P(),
            P(),
            P(("dp", "row"), "col"),
            P("col", ("dp", "row")),
        ),
        check_vma=False,
    )
```

profile of v0, /device:TPU:0, one launch (start us, length us, event | category | flops | bytes accessed | tf_op | source)
XLA Modules:
  0.0 2596.6 jit_solution(18329004856700081871)
XLA Ops:
  7.3 2582.2 %while.40 = (s32[]{:T(128)}, f32[48,384]{1,0:T(8,128)}, f32[48,384]{1,0:T(8,128)}, f32[48,384]{1,0:T(8,128)}, f32[48,1536]{1,0:T(8,128)}, /*index=5*/f32[384,48]...) while((s32[]{:T(128)}, f32[48,384]{1,0:T(8,128)}, ...), condition=%wide.region_45.46_spmd.clone, body=%wide.region_0.45_spmd.clone.sunk | while | flops 9846071296 | bytes 433621632 | solution.py:214
  13.9 47.7 %all_gather.108 = bf16[768,384]{1,0:T(8,128)(2,1)S(1)} all-gather(bf16[48,384]{1,0:T(8,128)(2,1)} %get-tuple-element.1002), channel_id=1, replica_groups=mesh['dp'=4,'row'=4,'col'=2] {'dp','row'}, dimensions={0}, use_global_device_ids=true | all-gather | bytes 626688 | tf_op jit(solution)/shard_map/while/body/eval_jaxpr/all_gather | solution.py:36
  69.9 46.9 %all_gather.110 = bf16[768,384]{1,0:T(8,128)(2,1)S(1)} all-gather(bf16[48,384]{1,0:T(8,128)(2,1)S(1)} %copy-done.37), channel_id=1, replica_groups=mesh['dp'=4,'row'=4,'col'=2] {'dp','row'}, dimensions={0}, use_global_device_ids=true | all-gather | bytes 626688 | tf_op jit(solution)/shard_map/while/body/eval_jaxpr/all_gather | solution.py:37
  119.0 47.4 %all_gather.107 = bf16[768,384]{1,0:T(8,128)(2,1)S(1)} all-gather(bf16[48,384]{1,0:T(8,128)(2,1)S(1)} %copy-done.36), channel_id=1, replica_groups=mesh['dp'=4,'row'=4,'col'=2] {'dp','row'}, dimensions={0}, use_global_device_ids=true | all-gather | bytes 626688 | tf_op jit(solution)/shard_map/while/body/eval_jaxpr/all_gather | solution.py:35
  168.0 44.4 %all_gather.112 = bf16[384,768]{0,1:T(8,128)(2,1)} all-gather(bf16[384,48]{0,1:T(8,128)(2,1)S(1)} %copy-done.38), channel_id=1, replica_groups=mesh['dp'=4,'row'=4,'col'=2] {'dp','row'}, dimensions={1}, use_global_device_ids=true | all-gather | bytes 626688 | tf_op jit(solution)/shard_map/while/body/eval_jaxpr/all_gather | solution.py:39
  246.0 60.3 %all-gather.13.cloned.1.call-done = bf16[768,1536]{1,0:T(8,128)(2,1)} async-done(((bf16[48,1536]{1,0:T(8,128)(2,1)}), bf16[768,1536]{1,0:T(8,128)(2,1)}) %all-gather.13.cloned.1.call-update) | async-done | bytes 2359312 | tf_op jit(solution)/shard_map/while/body/eval_jaxpr/all_gather | solution.py:38
  310.5 59.1 %all-gather.15.cloned.1.call-done = bf16[1536,768]{0,1:T(8,128)(2,1)} async-done(((bf16[1536,48]{0,1:T(8,128)(2,1)}), bf16[1536,768]{0,1:T(8,128)(2,1)}) %all-gather.15.cloned.1.call-update) | async-done | bytes 2359312 | tf_op jit(solution)/shard_map/while/body/eval_jaxpr/all_gather | solution.py:40
  492.6 120.5 %reduce-scatter.33.cloned.1.call-done = f32[384,48]{0,1:T(8,128)} async-done(((f32[384,768]{0,1:T(8,128)}), f32[384,48]{0,1:T(8,128)}) %reduce-scatter.33.cloned.1.call-update) | async-done | bytes 73744 | tf_op jit(solution)/shard_map/while/body/eval_jaxpr/reduce_scatter | solution.py:60
  614.1 128.5 %reduce-scatter.21.cloned.1.call-done = f32[48,384]{1,0:T(8,128)} async-done(((f32[768,384]{1,0:T(8,128)}), f32[48,384]{1,0:T(8,128)}) %reduce-scatter.21.cloned.1.call-update) | async-done | bytes 73744 | tf_op jit(solution)/shard_map/while/body/eval_jaxpr/reduce_scatter | solution.py:56
  797.3 86.0 %reduce-scatter.29.cloned.1.call-done = f32[48,384]{1,0:T(8,128)} async-done(((f32[768,384]{1,0:T(8,128)}), f32[48,384]{1,0:T(8,128)}) %reduce-scatter.29.cloned.1.call-update) | async-done | bytes 73744 | tf_op jit(solution)/shard_map/while/body/eval_jaxpr/reduce_scatter | solution.py:58
  884.2 128.4 %reduce-scatter.25.cloned.1.call-done = f32[48,384]{1,0:T(8,128)} async-done(((f32[768,384]{1,0:T(8,128)}), f32[48,384]{1,0:T(8,128)}) %reduce-scatter.25.cloned.1.call-update) | async-done | bytes 73744 | tf_op jit(solution)/shard_map/while/body/eval_jaxpr/reduce_scatter | solution.py:57
  1013.5 141.8 %reduce-scatter.35.cloned.1.call-done = f32[1536,48]{0,1:T(8,128)} async-done(((f32[1536,768]{0,1:T(8,128)}), f32[1536,48]{0,1:T(8,128)}) %reduce-scatter.35.cloned.1.call-update) | async-done | bytes 294928 | tf_op jit(solution)/shard_map/while/body/eval_jaxpr/reduce_scatter | solution.py:61
  1156.5 141.5 %reduce-scatter.31.cloned.1.call-done = f32[48,1536]{1,0:T(8,128)} async-done(((f32[768,1536]{1,0:T(8,128)}), f32[48,1536]{1,0:T(8,128)}) %reduce-scatter.31.cloned.1.call-update) | async-done | bytes 294928 | tf_op jit(solution)/shard_map/while/body/eval_jaxpr/reduce_scatter | solution.py:59
  1306.2 44.1 %all_gather.108 = bf16[768,384]{1,0:T(8,128)(2,1)S(1)} all-gather(bf16[48,384]{1,0:T(8,128)(2,1)} %get-tuple-element.1002), channel_id=1, replica_groups=mesh['dp'=4,'row'=4,'col'=2] {'dp','row'}, dimensions={0}, use_global_device_ids=true | all-gather | bytes 626688 | tf_op jit(solution)/shard_map/while/body/eval_jaxpr/all_gather | solution.py:36
  1358.6 46.8 %all_gather.110 = bf16[768,384]{1,0:T(8,128)(2,1)S(1)} all-gather(bf16[48,384]{1,0:T(8,128)(2,1)S(1)} %copy-done.37), channel_id=1, replica_groups=mesh['dp'=4,'row'=4,'col'=2] {'dp','row'}, dimensions={0}, use_global_device_ids=true | all-gather | bytes 626688 | tf_op jit(solution)/shard_map/while/body/eval_jaxpr/all_gather | solution.py:37
  1407.6 47.4 %all_gather.107 = bf16[768,384]{1,0:T(8,128)(2,1)S(1)} all-gather(bf16[48,384]{1,0:T(8,128)(2,1)S(1)} %copy-done.36), channel_id=1, replica_groups=mesh['dp'=4,'row'=4,'col'=2] {'dp','row'}, dimensions={0}, use_global_device_ids=true | all-gather | bytes 626688 | tf_op jit(solution)/shard_map/while/body/eval_jaxpr/all_gather | solution.py:35
  1535.0 60.2 %all-gather.13.cloned.1.call-done = bf16[768,1536]{1,0:T(8,128)(2,1)} async-done(((bf16[48,1536]{1,0:T(8,128)(2,1)}), bf16[768,1536]{1,0:T(8,128)(2,1)}) %all-gather.13.cloned.1.call-update) | async-done | bytes 2359312 | tf_op jit(solution)/shard_map/while/body/eval_jaxpr/all_gather | solution.py:38
  1599.4 59.2 %all-gather.15.cloned.1.call-done = bf16[1536,768]{0,1:T(8,128)(2,1)} async-done(((bf16[1536,48]{0,1:T(8,128)(2,1)}), bf16[1536,768]{0,1:T(8,128)(2,1)}) %all-gather.15.cloned.1.call-update) | async-done | bytes 2359312 | tf_op jit(solution)/shard_map/while/body/eval_jaxpr/all_gather | solution.py:40
  1781.6 120.5 %reduce-scatter.33.cloned.1.call-done = f32[384,48]{0,1:T(8,128)} async-done(((f32[384,768]{0,1:T(8,128)}), f32[384,48]{0,1:T(8,128)}) %reduce-scatter.33.cloned.1.call-update) | async-done | bytes 73744 | tf_op jit(solution)/shard_map/while/body/eval_jaxpr/reduce_scatter | solution.py:60
  1903.0 128.4 %reduce-scatter.21.cloned.1.call-done = f32[48,384]{1,0:T(8,128)} async-done(((f32[768,384]{1,0:T(8,128)}), f32[48,384]{1,0:T(8,128)}) %reduce-scatter.21.cloned.1.call-update) | async-done | bytes 73744 | tf_op jit(solution)/shard_map/while/body/eval_jaxpr/reduce_scatter | solution.py:56
  2086.3 86.0 %reduce-scatter.29.cloned.1.call-done = f32[48,384]{1,0:T(8,128)} async-done(((f32[768,384]{1,0:T(8,128)}), f32[48,384]{1,0:T(8,128)}) %reduce-scatter.29.cloned.1.call-update) | async-done | bytes 73744 | tf_op jit(solution)/shard_map/while/body/eval_jaxpr/reduce_scatter | solution.py:58
  2173.3 128.4 %reduce-scatter.25.cloned.1.call-done = f32[48,384]{1,0:T(8,128)} async-done(((f32[768,384]{1,0:T(8,128)}), f32[48,384]{1,0:T(8,128)}) %reduce-scatter.25.cloned.1.call-update) | async-done | bytes 73744 | tf_op jit(solution)/shard_map/while/body/eval_jaxpr/reduce_scatter | solution.py:57
  2302.6 141.6 %reduce-scatter.35.cloned.1.call-done = f32[1536,48]{0,1:T(8,128)} async-done(((f32[1536,768]{0,1:T(8,128)}), f32[1536,48]{0,1:T(8,128)}) %reduce-scatter.35.cloned.1.call-update) | async-done | bytes 294928 | tf_op jit(solution)/shard_map/while/body/eval_jaxpr/reduce_scatter | solution.py:61
  2445.3 142.4 %reduce-scatter.31.cloned.1.call-done = f32[48,1536]{1,0:T(8,128)} async-done(((f32[768,1536]{1,0:T(8,128)}), f32[48,1536]{1,0:T(8,128)}) %reduce-scatter.31.cloned.1.call-update) | async-done | bytes 294928 | tf_op jit(solution)/shard_map/while/body/eval_jaxpr/reduce_scatter | solution.py:59
  (537 shorter events, 523.0 us)
Async XLA Ops:
  7.3 205.5 %all-gather.9.cloned.1.call-start = ((), (), s32[]{:S(2)}) async-start(), calls=%async_computation.12 | async-start | bytes 1351680 | tf_op jit(solution)/shard_map/while/body/eval_jaxpr/all_gather | solution.py:103
  69.9 154.9 %all-gather.11.cloned.1.call-start = ((), (), s32[]{:S(2)}) async-start(), calls=%async_computation.13 | async-start | bytes 1351680 | tf_op jit(solution)/shard_map/while/body/eval_jaxpr/all_gather | solution.py:104
  118.9 121.4 %reduce-scatter.17.cloned.1.call-start = ((), (), s32[]{:S(2)}) async-start(), calls=%async_computation.14 | async-start | bytes 811008 | tf_op jit(solution)/shard_map/while/body/eval_jaxpr/reduce_scatter | solution.py:49
  235.8 133.7 %all-gather.15.cloned.1.call-start = ((), (), s32[]{:S(2)}) async-start(), calls=%async_computation.16 | async-start | bytes 2506752 | tf_op jit(solution)/shard_map/while/body/eval_jaxpr/all_gather | solution.py:40
  236.4 147.1 %reduce-scatter.19.cloned.1.call-start = ((), (), s32[]{:S(2)}) async-start(), calls=%async_computation.17 | async-start | bytes 811008 | tf_op jit(solution)/shard_map/while/body/eval_jaxpr/reduce_scatter | solution.py:49
  429.1 184.1 %reduce-scatter.33.cloned.1.call-start = ((), (), s32[]{:S(2)}) async-start(), calls=%async_computation.24 | async-start | bytes 1253376 | tf_op jit(solution)/shard_map/while/body/eval_jaxpr/reduce_scatter | solution.py:60
  431.8 310.8 %reduce-scatter.21.cloned.1.call-start = ((), (), s32[]{:S(2)}) async-start(), calls=%async_computation.18 | async-start | bytes 1253376 | tf_op jit(solution)/shard_map/while/body/eval_jaxpr/reduce_scatter | solution.py:56
  438.9 312.9 %reduce-scatter.37.cloned.1.call-start = ((), (), s32[]{:S(2)}) async-start(), calls=%async_computation.26 | async-start | bytes 811008 | tf_op jit(solution)/shard_map/while/body/eval_jaxpr/reduce_scatter | solution.py:49
  475.7 407.7 %reduce-scatter.29.cloned.1.call-start = ((), (), s32[]{:S(2)}) async-start(), calls=%async_computation.22 | async-start | bytes 1253376 | tf_op jit(solution)/shard_map/while/body/eval_jaxpr/reduce_scatter | solution.py:58
  477.4 535.2 %reduce-scatter.25.cloned.1.call-start = ((), (), s32[]{:S(2)}) async-start(), calls=%async_computation.20 | async-start | bytes 1253376 | tf_op jit(solution)/shard_map/while/body/eval_jaxpr/reduce_scatter | solution.py:57
  479.1 676.3 %reduce-scatter.35.cloned.1.call-start = ((), (), s32[]{:S(2)}) async-start(), calls=%async_computation.25 | async-start | bytes 5013504 | tf_op jit(solution)/shard_map/while/body/eval_jaxpr/reduce_scatter | solution.py:61
  484.5 813.5 %reduce-scatter.31.cloned.1.call-start = ((), (), s32[]{:S(2)}) async-start(), calls=%async_computation.23 | async-start | bytes 5013504 | tf_op jit(solution)/shard_map/while/body/eval_jaxpr/reduce_scatter | solution.py:59
  1299.8 200.8 %all-gather.9.cloned.1.call-start = ((), (), s32[]{:S(2)}) async-start(), calls=%async_computation.12 | async-start | bytes 1351680 | tf_op jit(solution)/shard_map/while/body/eval_jaxpr/all_gather | solution.py:103
  1358.6 154.0 %all-gather.11.cloned.1.call-start = ((), (), s32[]{:S(2)}) async-start(), calls=%async_computation.13 | async-start | bytes 1351680 | tf_op jit(solution)/shard_map/while/body/eval_jaxpr/all_gather | solution.py:104
  1407.5 121.8 %reduce-scatter.17.cloned.1.call-start = ((), (), s32[]{:S(2)}) async-start(), calls=%async_computation.14 | async-start | bytes 811008 | tf_op jit(solution)/shard_map/while/body/eval_jaxpr/reduce_scatter | solution.py:49
  1523.6 135.0 %all-gather.15.cloned.1.call-start = ((), (), s32[]{:S(2)}) async-start(), calls=%async_computation.16 | async-start | bytes 2506752 | tf_op jit(solution)/shard_map/while/body/eval_jaxpr/all_gather | solution.py:40
  1524.3 148.2 %reduce-scatter.19.cloned.1.call-start = ((), (), s32[]{:S(2)}) async-start(), calls=%async_computation.17 | async-start | bytes 811008 | tf_op jit(solution)/shard_map/while/body/eval_jaxpr/reduce_scatter | solution.py:49
  1718.2 183.9 %reduce-scatter.33.cloned.1.call-start = ((), (), s32[]{:S(2)}) async-start(), calls=%async_computation.24 | async-start | bytes 1253376 | tf_op jit(solution)/shard_map/while/body/eval_jaxpr/reduce_scatter | solution.py:60
  1720.9 310.6 %reduce-scatter.21.cloned.1.call-start = ((), (), s32[]{:S(2)}) async-start(), calls=%async_computation.18 | async-start | bytes 1253376 | tf_op jit(solution)/shard_map/while/body/eval_jaxpr/reduce_scatter | solution.py:56
  1728.0 312.8 %reduce-scatter.37.cloned.1.call-start = ((), (), s32[]{:S(2)}) async-start(), calls=%async_computation.26 | async-start | bytes 811008 | tf_op jit(solution)/shard_map/while/body/eval_jaxpr/reduce_scatter | solution.py:49
  1764.6 407.8 %reduce-scatter.29.cloned.1.call-start = ((), (), s32[]{:S(2)}) async-start(), calls=%async_computation.22 | async-start | bytes 1253376 | tf_op jit(solution)/shard_map/while/body/eval_jaxpr/reduce_scatter | solution.py:58
  1766.3 535.3 %reduce-scatter.25.cloned.1.call-start = ((), (), s32[]{:S(2)}) async-start(), calls=%async_computation.20 | async-start | bytes 1253376 | tf_op jit(solution)/shard_map/while/body/eval_jaxpr/reduce_scatter | solution.py:57
  1768.0 676.2 %reduce-scatter.35.cloned.1.call-start = ((), (), s32[]{:S(2)}) async-start(), calls=%async_computation.25 | async-start | bytes 5013504 | tf_op jit(solution)/shard_map/while/body/eval_jaxpr/reduce_scatter | solution.py:61
  1773.4 814.3 %reduce-scatter.31.cloned.1.call-start = ((), (), s32[]{:S(2)}) async-start(), calls=%async_computation.23 | async-start | bytes 5013504 | tf_op jit(solution)/shard_map/while/body/eval_jaxpr/reduce_scatter | solution.py:59
  (126 other events, 19391.1 us)
Sparse Core Ops, SparseCore 0:
  70.0 31.1 all-gather.8
  119.0 31.0 all-gather.10
  242.9 63.3 all-gather.12
  308.9 60.6 all-gather.14
  415.4 28.8 reduce-scatter.22
  446.7 26.3 reduce-scatter.26
  486.4 126.7 reduce-scatter.32
  617.9 124.6 reduce-scatter.20
  756.5 126.7 reduce-scatter.28
  887.9 124.6 reduce-scatter.24
  1017.6 137.7 reduce-scatter.34
  1160.4 137.5 reduce-scatter.30
  1358.7 31.2 all-gather.8
  1407.6 31.4 all-gather.10
  1531.9 63.2 all-gather.12
  1597.9 60.6 all-gather.14
  1704.5 28.8 reduce-scatter.22
  1735.6 26.3 reduce-scatter.26
  1775.3 126.6 reduce-scatter.32
  1906.7 124.7 reduce-scatter.20
  2045.5 126.7 reduce-scatter.28
  2177.0 124.6 reduce-scatter.24
  2306.8 137.3 reduce-scatter.34
  2449.4 138.2 reduce-scatter.30
  (8 shorter events, 50.2 us)
where the time goes:
time: 2600 us
  waiting for transfers between devices  1820 us (70%)
  blocking collectives  468 us (18%)
  matrix products  170 us (7%)
  other arithmetic  64.8 us (2%)
  local copies, waits for them, and re-layouts  58.7 us (2%)
    reduce_scatter x2, waiting for transfers between devices, reduce_grads(): lax.psum_scatter(weight_part[3], ('dp', 'row'), scatter_dimension=0, tile...  284 us
    reduce_scatter x2, waiting for transfers between devices, reduce_grads(): lax.psum_scatter(weight_part[5], ('dp', 'row'), scatter_dimension=1, tile...  283 us
    reduce_scatter x2, waiting for transfers between devices, reduce_grads(): lax.psum_scatter(weight_part[0], ('dp', 'row'), scatter_dimension=0, tile...  257 us
    reduce_scatter x2, waiting for transfers between devices, reduce_grads(): lax.psum_scatter(weight_part[1], ('dp', 'row'), scatter_dimension=0, tile...  257 us
    reduce_scatter x2, waiting for transfers between devices, reduce_grads(): lax.psum_scatter(weight_part[4], ('dp', 'row'), scatter_dimension=1, tile...  241 us
    reduce_scatter x2, waiting for transfers between devices, reduce_grads(): lax.psum_scatter(weight_part[2], ('dp', 'row'), scatter_dimension=0, tile...  172 us
    all_gather x2, waiting for transfers between devices, fetch(): lax.all_gather(blocks[3], ('dp', 'row'), axis=0, tiled=True)  120 us
    all_gather x2, waiting for transfers between devices, fetch(): lax.all_gather(blocks[5], ('dp', 'row'), axis=1, tiled=True)  118 us
  transfers between devices with their start and end apart: 32, of which 26 were waited for; matrix products, arithmetic and copies ran while one was open for 6% of the time, Pallas kernels for 0%

commit v1 on v0

v1 whole, which is shorter than its diff:
```python
import functools
import math

import jax
import jax.numpy as jnp
from jax import lax
from jax.experimental import pallas as pl
from jax.experimental.pallas import tpu as pltpu
from jax.sharding import PartitionSpec as P

HD = 64
LANES = 128
TILE = 256
EPSILON = 1e-06
BF = jnp.bfloat16
F4 = jnp.float32
VM = pl.BlockSpec(memory_space=pltpu.VMEM)


def ring_order(n):
    return list(range(0, n, 2)) + list(range(n - 1 - (n % 2), 0, -2))


def ring_place(r, n):
    return jnp.where(r % 2 == 0, r // 2, n - 1 - r // 2 - (n % 2) + (n % 2) * 1)


def ring_row(q, n):
    return jnp.where(2 * q < n, 2 * q, 2 * (n - 1 - q) + 1)


def hop(x, n):
    order = ring_order(n)
    pairs = [(order[i], order[(i + 1) % n]) for i in range(n)]
    return lax.ppermute(x, "row", pairs)


def swap_bit(x, axis, n, bit):
    return lax.ppermute(x, axis, [(i, i ^ (1 << bit)) for i in range(n)])


def swap_core(x):
    return lax.ppermute(x, "col", [(0, 1), (1, 0)])


def bit_orders(n):
    bits = list(range(n.bit_length() - 1))
    half = len(bits) // 2
    return bits, bits[half:] + bits[:half]


def regular(block):
    dp = lax.axis_size("dp")
    return dp & (dp - 1) == 0 and block % 16 == 0


def gather_line(shard):
    n = lax.axis_size("row")
    place = ring_place(lax.axis_index("row"), n)
    blocks = [shard]
    for _ in range(n - 1):
        blocks.append(hop(blocks[-1], n))
    parts = []
    for r in range(n):
        slot = (place - ring_order(n).index(r)) % n
        parts.append(lax.select_n(slot, *blocks) if n > 1 else blocks[0])
    return jnp.concatenate(parts, axis=0)


def gather_plane(x, order):
    n = lax.axis_size("dp")
    me = lax.axis_index("dp")
    done = []
    for bit in order:
        other = swap_bit(x, "dp", n, bit)
        at = sum(1 for b in done if b > bit)
        low = (me >> bit) & 1
        first = jnp.where(low == 0, x, other)
        second = jnp.where(low == 0, other, x)
        x = jnp.stack([first, second], axis=at)
        done.append(bit)
    return x.reshape(-1, x.shape[-1])


def gather_weights(shard, cut):
    block = shard.shape[0]
    if not regular(block):
        whole = lax.all_gather(shard, ("dp", "row"), axis=0, tiled=True)
        one, two = whole[:, :cut], whole[:, cut:]
    else:
        line = gather_line(shard)
        a, b = bit_orders(lax.axis_size("dp"))
        one = gather_plane(line[:, :cut], a)
        two = gather_plane(line[:, cut:], b)
    return (one, swap_core(one)), (two, swap_core(two))


def add_low(a, b):
    return (a.astype(F4) + b.astype(F4)).astype(BF)


def scatter_plane(x, order):
    n = lax.axis_size("dp")
    me = lax.axis_index("dp")
    count = n.bit_length() - 1
    x = x.reshape((2,) * count + (-1, x.shape[-1]))
    left = list(range(count - 1, -1, -1))
    for bit in order:
        at = left.index(bit)
        low = (me >> bit) & 1
        send = lax.dynamic_index_in_dim(x, 1 - low, at, keepdims=False)
        keep = lax.dynamic_index_in_dim(x, low, at, keepdims=False)
        x = add_low(keep, swap_bit(send, "dp", n, bit))
        left.remove(bit)
    return x


def scatter_line(x):
    n = lax.axis_size("row")
    place = ring_place(lax.axis_index("row"), n)
    x = x.reshape(n, -1, x.shape[-1])

    def own(q):
        return lax.dynamic_index_in_dim(x, ring_row(q % n, n), 0, keepdims=False)

    if n == 1:
        return x[0].astype(F4)
    acc = own(place - 1 + n)
    for step in range(n - 2):
        acc = add_low(own(place - 2 - step + n), hop(acc, n))
    return own(place).astype(F4) + hop(acc, n).astype(F4)


def scatter_grads(one, two):
    block = one[0].shape[0] // (lax.axis_size("dp") * lax.axis_size("row"))
    one = add_low(one[0], swap_core(one[1]))
    two = add_low(two[0], swap_core(two[1]))
    if not regular(block):
        both = jnp.concatenate([one, two], axis=1)
        return lax.psum_scatter(
            both, ("dp", "row"), scatter_dimension=0, tiled=True
        ).astype(F4)
    a, b = bit_orders(lax.axis_size("dp"))
    both = jnp.concatenate([scatter_plane(one, a), scatter_plane(two, b)], axis=1)
    return scatter_line(both)


def sum_all(x):
    x = x + swap_core(x)
    for axis in ("dp", "row"):
        n = lax.axis_size(axis)
        if n & (n - 1):
            x = lax.psum(x, axis)
        else:
            for bit in range(n.bit_length() - 1):
                x = x + swap_bit(x, axis, n, bit)
    return x


def dot_nn(a, b):
    return jnp.dot(a, b, preferred_element_type=F4)


def dot_nt(a, b):
    return lax.dot_general(a, b, (((1,), (1,)), ((), ())), preferred_element_type=F4)


def dot_tn(a, b):
    return lax.dot_general(a, b, (((0,), (0,)), ((), ())), preferred_element_type=F4)


def mean_last(x):
    return jnp.mean(x, axis=-1, keepdims=True)


def centre(x):
    c = x - mean_last(x)
    return c, lax.rsqrt(mean_last(c * c) + EPSILON)


def group_matrix():
    i = lax.broadcasted_iota(jnp.int32, (TILE, TILE), 0) // HD
    j = lax.broadcasted_iota(jnp.int32, (TILE, TILE), 1) // HD
    return jnp.where(i == j, 1.0 / HD, 0.0).astype(BF)


def group_mean(x, matrix):
    high = x.astype(BF)
    low = (x - high.astype(F4)).astype(BF)
    return dot_nn(high, matrix) + dot_nn(low, matrix)


def head_norm(x, matrix):
    c = x - group_mean(x, matrix)
    return c, lax.rsqrt(group_mean(c * c, matrix) + EPSILON)


def head_norm_back(e, x, gain, matrix):
    c, r = head_norm(x, matrix)
    t = e * gain
    d = r * (t - group_mean(t, matrix) - c * (r * r) * group_mean(t * c, matrix))
    return d, e * c * r


def fold_heads(x):
    return jnp.sum(x, axis=0, keepdims=True)


def tiles(width):
    return width // TILE


def lane(i, width):
    return pl.ds(pl.multiple_of(i * width, width), width)


def call(body, outs, scratch, flops, *args):
    size = sum(a.size * a.dtype.itemsize for a in args)
    size += sum(math.prod(s) * jnp.dtype(d).itemsize for s, d in outs)
    hold = sum(math.prod(s.shape) * jnp.dtype(s.dtype).itemsize for s in scratch)
    limit = min(62 << 20, size + hold + (12 << 20))
    return pl.pallas_call(
        body,
        out_shape=[jax.ShapeDtypeStruct(s, d) for s, d in outs],
        in_specs=[VM] * len(args),
        out_specs=[VM] * len(outs),
        scratch_shapes=scratch,
        compiler_params=pltpu.CompilerParams(vmem_limit_bytes=limit),
        cost_estimate=pl.CostEstimate(
            flops=int(flops), bytes_accessed=int(size), transcendentals=0
        ),
    )(*args)


def qkv_body(with_query, half, *refs):
    p, g1, b1, qg, kg, a1o, a1x, a2o, a2x = refs[:9]
    normed, k_raw, k_low, v_low = refs[9:13]
    x = p[...].astype(F4)
    c, r = centre(x)
    n = (c * r * g1[...] + b1[...]).astype(BF)
    normed[...] = n
    head = 0 if with_query else half
    cut = a1o.shape[1]
    for s, (a1, a2) in enumerate(((a1o, a2o), (a1x, a2x))):
        at = s * half
        one = dot_nn(n, a1[:, head:])
        two = dot_nn(n, a2[...])
        if with_query:
            refs[13][:, at : at + half] = one[:, :half]
        k_raw[:, at : at + cut - half] = one[:, half - head :]
        k_raw[:, at + cut - half : at + half] = two[:, : 2 * half - cut]
        v_low[:, at : at + half] = two[:, 2 * half - cut :].astype(BF)
    matrix = group_matrix()
    for t in range(tiles(2 * half)):
        cols = slice(t * TILE, (t + 1) * TILE)
        c, r = head_norm(k_raw[:, cols], matrix)
        k_low[:, cols] = (c * r * kg[...]).astype(BF)
        if with_query:
            c, r = head_norm(refs[13][:, cols], matrix)
            refs[14][:, cols] = (c * r * qg[...] * (float(HD) ** -0.5)).astype(BF)


def qkv_block(with_query, p, g1, b1, qg, kg, parts):
    tokens, width = p.shape
    half = width // 2
    outs = [((tokens, width), BF), ((tokens, width), F4)] + [((tokens, width), BF)] * 2
    if with_query:
        outs += [((tokens, width), F4), ((tokens, width), BF)]
    flops = 2 * tokens * width * width * (3 if with_query else 2)
    body = functools.partial(qkv_body, with_query, half)
    return call(body, outs, [], flops, p, g1, b1, qg, kg, *parts)


def pair_masks(rows):
    at = lax.broadcasted_iota(jnp.int32, (rows, LANES), 1)
    return (at < HD, at >= HD)


def pick(x, mask):
    return jnp.where(mask, x, jnp.zeros_like(x))


def column(ref, h):
    at = lax.broadcasted_iota(jnp.int32, ref.shape, 1)
    return jnp.sum(jnp.where(at == h, ref[...], 0.0), axis=-1, keepdims=True)


def attend_body(n, *refs):
    q, idq, idk = refs[:3]
    ks, vs = refs[3 : 3 + n], refs[3 + n : 3 + 2 * n]
    att, stat, k_all, v_all, bias = refs[3 + 2 * n :]
    tokens = q.shape[0]
    for b in range(n):
        k_all[b * tokens : (b + 1) * tokens, :] = ks[b][...]
        v_all[b * tokens : (b + 1) * tokens, :] = vs[b][...]
    bias[...] = jnp.where(idq[...] == idk[...], 0.0, -1e30)
    stat[...] = jnp.zeros_like(stat)
    masks = pair_masks(tokens)
    at = lax.broadcasted_iota(jnp.int32, stat.shape, 1)

    @pl.loop(0, q.shape[1] // LANES)
    def _(pair):
        cols = lane(pair, LANES)
        q_pair = q[:, cols]
        k_pair = k_all[:, cols]
        v_pair = v_all[:, cols]
        outs = []
        for s, mask in enumerate(masks):
            e = jnp.exp(dot_nt(pick(q_pair, mask), k_pair) + bias[...])
            total = jnp.sum(e, axis=-1, keepdims=True)
            low = (e * (1.0 / total)).astype(BF)
            outs.append(dot_nn(low, v_pair))
            stat[...] += jnp.where(at == 2 * pair + s, jnp.log(total), 0.0)
        att[:, cols] = jnp.where(masks[0], outs[0], outs[1]).astype(BF)


def attend(q, idq, idk, ks, vs):
    tokens, width = q.shape
    n = len(ks)
    outs = [((tokens, width), BF), ((tokens, LANES), F4)]
    scratch = [
        pltpu.VMEM((n * tokens, width), BF),
        pltpu.VMEM((n * tokens, width), BF),
        pltpu.VMEM((tokens, n * tokens), F4),
    ]
    flops = 4 * tokens * n * tokens * width * 4
    body = functools.partial(attend_body, n)
    return call(body, outs, scratch, flops, q, idq, idk, *ks, *vs)


ROOT = math.sqrt(2.0 / math.pi)
CUBE = 0.044715


def gelu_pair(u):
    square = u * u
    t = jnp.tanh(ROOT * u * (1.0 + CUBE * square))
    half = 0.5 * (1.0 + t)
    slope = half + 0.5 * u * (1.0 - t * t) * (ROOT * (1.0 + 3.0 * CUBE * square))
    return u * half, slope


def up_body(half, p, att, cot, g2, b2, b1o, b1x, b2o, b2x, *outs):
    mixed, n2, act, slope, g1o, g1x, g2o, g2x = outs
    first = b1o.shape[1]
    inner = first + b2o.shape[1] - half
    m = p[...].astype(F4)
    for s, part in enumerate((b2o, b2x)):
        m = m + dot_nt(att[:, s * half : (s + 1) * half], part[:, :half])
    mixed[...] = m
    c, r = centre(m)
    n2[...] = (c * r * g2[...] + b2[...]).astype(BF)
    for s, (one, two) in enumerate(((b1o, b2o), (b1x, b2x))):

        @pl.loop(0, tiles(first))
        def _(i):
            u = dot_nn(n2[...], one[:, lane(i, TILE)])
            to = pl.ds(pl.multiple_of(s * inner + i * TILE, TILE), TILE)
            a, d = gelu_pair(u)
            act[:, to] = a.astype(BF)
            slope[:, to] = d.astype(BF)

        rest = inner - first
        for i in range(tiles(rest)):
            u = dot_nn(n2[...], two[:, half + i * TILE : half + (i + 1) * TILE])
            to = slice(s * inner + first + i * TILE, s * inner + first + (i + 1) * TILE)
            a, d = gelu_pair(u)
            act[:, to] = a.astype(BF)
            slope[:, to] = d.astype(BF)
    mid = g1o.shape[1]
    for s, (one, two) in enumerate(((g1o, g2o), (g1x, g2x))):
        for base, out in ((s * inner, one), (s * inner + mid, two)):

            @pl.loop(0, tiles(mid))
            def _(i):
                frm = pl.ds(pl.multiple_of(base + i * TILE, TILE), TILE)
                out[:, lane(i, TILE)] = dot_tn(cot[...], act[:, frm]).astype(BF)


def down_body(half, *refs):
    mixed, n2, act, slope, att, cot, g2 = refs[:7]
    b1o, b1x, b2o, b2x, c1o, c1x, c2o, c2x = refs[7:15]
    result, d_mixed, d_att, delta, gains, h1o, h1x, h2o, h2x, d_up = refs[15:]
    first = b1o.shape[1]
    inner = first + b2o.shape[1] - half
    mid = c1o.shape[1]
    out = mixed[...]
    for s, (one, two) in enumerate(((c1o, c2o), (c1x, c2x))):
        at = s * inner
        out = out + dot_nt(act[:, at : at + mid], one[...])
        out = out + dot_nt(act[:, at + mid : at + inner], two[...])
        for base, part in ((at, one), (at + mid, two)):

            @pl.loop(0, tiles(mid))
            def _(i):
                to = pl.ds(pl.multiple_of(base + i * TILE, TILE), TILE)
                d = dot_nn(cot[...], part[:, lane(i, TILE)])
                d_up[:, to] = (d * slope[:, to].astype(F4)).astype(BF)

    result[...] = out.astype(BF)
    e = jnp.zeros(mixed.shape, F4)
    for s, (one, two) in enumerate(((b1o, b2o), (b1x, b2x))):
        at = s * inner
        e = e + dot_nt(d_up[:, at : at + first], one[...])
        e = e + dot_nt(d_up[:, at + first : at + inner], two[:, half:])
    c, r = centre(mixed[...])
    t = e * g2[...]
    d_mixed[...] = cot[...].astype(F4) + r * (
        t - mean_last(t) - c * (r * r) * mean_last(t * c)
    )
    gains[0:1, :] = jnp.sum(e * c * r, axis=0, keepdims=True)
    gains[1:2, :] = jnp.sum(e, axis=0, keepdims=True)
    d_branch = d_mixed[...].astype(BF)
    row = lax.broadcasted_iota(jnp.int32, (half, LANES), 0) // HD
    col = lax.broadcasted_iota(jnp.int32, (half, LANES), 1)
    sums = jnp.zeros(delta.shape, F4)
    for s, part in enumerate((b2o, b2x)):
        cols = slice(s * half, (s + 1) * half)
        d = dot_nn(d_branch, part[:, :half]).astype(BF)
        d_att[:, cols] = d
        prod = d.astype(F4) * att[:, cols].astype(F4)
        high = prod.astype(BF)
        low = (prod - high.astype(F4)).astype(BF)
        sel = jnp.where(row + s * (half // HD) == col, 1.0, 0.0).astype(BF)
        sums = sums + dot_nn(high, sel) + dot_nn(low, sel)
    delta[...] = sums
    for s, (one, two) in enumerate(((h1o, h2o), (h1x, h2x))):
        at = s * inner
        two[:, :half] = dot_tn(d_branch, att[:, s * half : (s + 1) * half]).astype(BF)

        @pl.loop(0, tiles(first))
        def _(i):
            frm = pl.ds(pl.multiple_of(at + i * TILE, TILE), TILE)
            one[:, lane(i, TILE)] = dot_tn(n2[...], d_up[:, frm]).astype(BF)

        two[:, half:] = dot_tn(n2[...], d_up[:, at + first : at + inner]).astype(BF)


def back_body(half, *refs):
    q, k, v, d_att, stat, delta, idq, idk, k_raw, p, kg = refs[:11]
    a1o, a1x, a2o, a2x = refs[11:15]
    dk_low, dv_low, dq, part, k_gain, gains, bias, dk = refs[15:]
    tokens = q.shape[0]
    bias[...] = jnp.where(idq[...] == idk[...], 0.0, -1e30)
    masks = pair_masks(tokens)

    @pl.loop(0, q.shape[1] // LANES)
    def _(pair):
        cols = lane(pair, LANES)
        q_pair, k_pair, v_pair, d_pair = q[:, cols], k[:, cols], v[:, cols], d_att[:, cols]
        sum_q = sum_k = sum_v = None
        for s, mask in enumerate(masks):
            q_one, d_one, k_one = pick(q_pair, mask), pick(d_pair, mask), pick(k_pair, mask)
            h = 2 * pair + s
            score = dot_nt(q_one, k_pair) + bias[...]
            prob = jnp.exp(score - column(stat, h))
            d_prob = dot_nt(d_one, v_pair)
            d_score = (prob * (d_prob - column(delta, h))).astype(BF)
            one_v = dot_tn(prob.astype(BF), d_one)
            one_k = dot_tn(d_score, q_one)
            one_q = dot_nn(d_score, k_one)
            sum_v = one_v if s == 0 else sum_v + one_v
            sum_k = one_k if s == 0 else sum_k + one_k
            sum_q = one_q if s == 0 else sum_q + one_q
        dq[:, cols] = sum_q
        dk[:, cols] = sum_k
        dv_low[:, cols] = sum_v.astype(BF)

    matrix = group_matrix()
    total = jnp.zeros((1, TILE), F4)
    for t in range(tiles(2 * half)):
        cols = slice(t * TILE, (t + 1) * TILE)
        d, g = head_norm_back(dk[:, cols], k_raw[:, cols], kg[...], matrix)
        dk_low[:, cols] = d.astype(BF)
        total = total + fold_heads(g)
    k_gain[...] = total
    cut = a1o.shape[1]
    e = jnp.zeros((tokens, 2 * half), F4)
    for s, (one, two) in enumerate(((a1o, a2o), (a1x, a2x))):
        at = s * half
        mid = at + cut - half
        e = e + dot_nt(dk_low[:, at:mid], one[:, half:])
        e = e + dot_nt(dk_low[:, mid : at + half], two[:, : 2 * half - cut])
        e = e + dot_nt(dv_low[:, at : at + half], two[:, 2 * half - cut :])
    part[...] = e.astype(part.dtype)
    c, r = centre(p[...].astype(F4))
    gains[0:1, :] = jnp.sum(e * c * r, axis=0, keepdims=True)
    gains[1:2, :] = jnp.sum(e, axis=0, keepdims=True)


def back_block(last, q, k, v, d_att, stat, delta, idq, idk, k_raw, p, kg, parts):
    tokens, width = q.shape
    half = width // 2
    outs = [
        ((tokens, width), BF),
        ((tokens, width), BF),
        ((tokens, width), F4),
        ((tokens, width), F4 if last else BF),
        ((1, TILE), F4),
        ((2, width), F4),
    ]
    scratch = [pltpu.VMEM((tokens, tokens), F4), pltpu.VMEM((tokens, width), F4)]
    flops = 10 * tokens * tokens * width * 4 + 4 * tokens * width * width
    body = functools.partial(back_body, half)
    return call(
        body, outs, scratch, flops,
        q, k, v, d_att, stat, delta, idq, idk, k_raw, p, kg, *parts,
    )


def weight_body(n, half, *refs):
    q_raw, qg, p, own = refs[:4]
    a1o, a1x = refs[4:6]
    dqs, ns = refs[6 : 6 + n], refs[6 + n : 6 + 2 * n]
    dks, dvs = refs[6 + 2 * n : 6 + 3 * n], refs[6 + 3 * n : 6 + 4 * n]
    part, q_gain, gains, g1o, g1x, g2o, g2x, dq_low, n_all, dk_all, dv_all = refs[6 + 4 * n :]
    tokens = q_raw.shape[0]
    matrix = group_matrix()
    total = jnp.zeros((1, TILE), F4)
    factor = float(HD) ** -0.5
    for t in range(tiles(2 * half)):
        cols = slice(t * TILE, (t + 1) * TILE)
        e = dqs[0][:, cols]
        for other in dqs[1:]:
            e = e + other[:, cols]
        d, g = head_norm_back(e * factor, q_raw[:, cols], qg[...], matrix)
        dq_low[:, cols] = d.astype(BF)
        total = total + fold_heads(g)
    q_gain[...] = total
    e = dot_nt(dq_low[:, :half], a1o[:, :half]) + dot_nt(dq_low[:, half:], a1x[:, :half])
    part[...] = own[...] + e
    c, r = centre(p[...].astype(F4))
    gains[0:1, :] = jnp.sum(e * c * r, axis=0, keepdims=True)
    gains[1:2, :] = jnp.sum(e, axis=0, keepdims=True)
    for b in range(n):
        rows = slice(b * tokens, (b + 1) * tokens)
        n_all[rows, :] = ns[b][...]
        dk_all[rows, :] = dks[b][...]
        dv_all[rows, :] = dvs[b][...]
    cut = g1o.shape[1]
    for s, (one, two) in enumerate(((g1o, g2o), (g1x, g2x))):
        at = s * half
        mid = at + cut - half
        one[:, :half] = dot_tn(ns[0][...], dq_low[:, at : at + half]).astype(BF)
        one[:, half:] = dot_tn(n_all[...], dk_all[:, at:mid]).astype(BF)
        two[:, : 2 * half - cut] = dot_tn(n_all[...], dk_all[:, mid : at + half]).astype(BF)
        two[:, 2 * half - cut :] = dot_tn(n_all[...], dv_all[:, at : at + half]).astype(BF)


def take_micro(x, c):
    mine = jnp.where(c == 0, x[0], x[1])
    other = jnp.where(c == 0, x[1], x[0])
    return mine, other


def per_device(
    patches,
    picture_ids,
    ln1_gain,
    ln1_bias,
    w_query,
    w_key,
    w_value,
    q_gain,
    k_gain,
    w_out,
    ln2_gain,
    ln2_bias,
    w_up,
    w_down,
    cotangent,
):
    n = lax.axis_size("row")
    c = lax.axis_index("col")
    place = ring_place(lax.axis_index("row"), n)
    width = patches.shape[-1]
    half = w_query.shape[1]
    piece = patches.shape[2]
    tokens = 2 * piece
    inner = w_up.shape[1]

    both = jnp.stack([patches[0], cotangent[0]], axis=1)
    mine, other = take_micro(both, c)
    got = swap_core(other)
    low = jnp.where(c == 0, mine, got)
    high = jnp.where(c == 0, got, mine)
    own = jnp.concatenate([low, high], axis=1)
    p_own, cot = own[0], own[1]

    cut_a = half + half * 2 // 3
    first = inner * 2 // 3
    chunk_a = jnp.concatenate([w_query, w_key, w_value], axis=1)
    chunk_b = jnp.concatenate([w_up[:, :first], w_out.T, w_up[:, first:]], axis=1)
    chunk_c = w_down.T
    a_one, a_two = gather_weights(chunk_a, cut_a)
    a_parts = a_one + a_two
    blocks = [p_own]
    for _ in range(n - 1):
        blocks.append(hop(blocks[-1], n))
    b_one, b_two = gather_weights(chunk_b, first)
    b_parts = b_one + b_two
    c_one, c_two = gather_weights(chunk_c, inner // 2)
    c_parts = c_one + c_two

    g1, b1 = ln1_gain[None], ln1_bias[None]
    g2, b2 = ln2_gain[None], ln2_bias[None]
    qg, kg = jnp.tile(q_gain, TILE // HD)[None], jnp.tile(k_gain, TILE // HD)[None]

    ids = jnp.where(c == 0, picture_ids[0, 0], picture_ids[0, 1]).reshape(n, tokens)
    id_blocks = [
        lax.dynamic_index_in_dim(ids, ring_row((place - j + n) % n, n), 0)
        for j in range(n)
    ]
    idq = id_blocks[0].reshape(tokens, 1)
    idk = jnp.concatenate(id_blocks, axis=1)

    made = [qkv_block(j == 0, blocks[j], g1, b1, qg, kg, a_parts) for j in range(n)]
    q_raw, q_low = made[0][4], made[0][5]
    normed = [m[0] for m in made]
    k_raw, k_low, v_low = [m[1] for m in made], [m[2] for m in made], [m[3] for m in made]

    att, stat = attend(q_low, idq, idk, k_low, v_low)

    mid = inner // 2
    mixed, n2, act, slope, *gc = call(
        functools.partial(up_body, half),
        [((tokens, width), F4), ((tokens, width), BF)]
        + [((tokens, 2 * inner), BF)] * 2
        + [((width, mid), BF)] * 4,
        [],
        2 * tokens * width * (width + 4 * inner),
        p_own, att, cot, g2, b2, *b_parts,
    )
    grad_c = scatter_grads((gc[0], gc[1]), (gc[2], gc[3]))

    result, d_mixed, d_att, delta, gains2, *gb = call(
        functools.partial(down_body, half),
        [((tokens, width), BF), ((tokens, width), F4), ((tokens, width), BF)]
        + [((tokens, LANES), F4), ((2, width), F4)]
        + [((width, first), BF)] * 2
        + [((width, half + inner - first), BF)] * 2,
        [pltpu.VMEM((tokens, 2 * inner), BF)],
        2 * tokens * width * (2 * width + 8 * inner),
        mixed, n2, act, slope, att, cot, g2, *b_parts, *c_parts,
    )
    grad_b = scatter_grads((gb[0], gb[1]), (gb[2], gb[3]))

    back = [None] * n
    acc = None
    for j in [*range(1, n), 0]:
        back[j] = back_block(
            j == 0, q_low, k_low[j], v_low[j], d_att, stat, delta, idq,
            id_blocks[j], k_raw[j], blocks[j], kg, a_parts,
        )
        if j:
            part = back[j][3]
            acc = part if acc is None else add_low(part, acc)
            acc = hop(acc, n)

    part, dq_gain, gains_q, *ga = call(
        functools.partial(weight_body, n, half),
        [((tokens, width), F4), ((1, TILE), F4), ((2, width), F4)]
        + [((width, cut_a), BF)] * 2
        + [((width, 3 * half - cut_a), BF)] * 2,
        [pltpu.VMEM((tokens, width), BF)] + [pltpu.VMEM((n * tokens, width), BF)] * 3,
        2 * tokens * width * width * (2 + 2 * n),
        q_raw, qg, p_own, back[0][3], *a_one,
        *[b[2] for b in back], *normed, *[b[0] for b in back], *[b[1] for b in back],
    )
    grad_a = scatter_grads((ga[0], ga[1]), (ga[2], ga[3]))

    gains1 = gains_q
    key_gain = jnp.zeros((1, TILE), F4)
    for b in back:
        gains1 = gains1 + b[5]
        key_gain = key_gain + b[4]
    small = jnp.concatenate(
        [
            gains1.reshape(-1, LANES),
            gains2.reshape(-1, LANES),
            dq_gain.reshape(-1, LANES),
            key_gain.reshape(-1, LANES),
        ],
        axis=0,
    )
    small = sum_all(small)
    step = width // LANES
    grad_g1, grad_b1 = small[:step].reshape(-1), small[step : 2 * step].reshape(-1)
    grad_g2, grad_b2 = (
        small[2 * step : 3 * step].reshape(-1),
        small[3 * step : 4 * step].reshape(-1),
    )
    rest = TILE // LANES
    grad_gq = small[4 * step : 4 * step + rest].reshape(-1, HD).sum(axis=0)
    grad_gk = small[4 * step + rest :].reshape(-1, HD).sum(axis=0)

    e = part if acc is None else part + acc.astype(F4)
    centred, rate = centre(p_own.astype(F4))
    t = e * g1
    grad_in = d_mixed + rate * (
        t - mean_last(t) - centred * (rate * rate) * mean_last(t * centred)
    )

    def back_home(x):
        lower, upper = x[:piece], x[piece:]
        keep = jnp.where(c == 0, lower, upper)
        got = swap_core(jnp.where(c == 0, upper, lower))
        return jnp.stack([jnp.where(c == 0, keep, got), jnp.where(c == 0, got, keep)])

    rest = half + first
    grad_wu = jnp.concatenate([grad_b[:, :first], grad_b[:, rest:]], axis=1)
    return (
        back_home(result)[None],
        back_home(grad_in)[None],
        grad_g1,
        grad_b1,
        grad_a[:, :half],
        grad_a[:, half : 2 * half],
        grad_a[:, 2 * half :],
        grad_gq,
        grad_gk,
        grad_b[:, first:rest].T,
        grad_g2,
        grad_b2,
        grad_wu,
        grad_c.T,
    )


def solution(mesh):
    rows = P("dp", None, ("row", "col"), None)
    inward = P(("dp", "row"), "col")
    outward = P("col", ("dp", "row"))
    return jax.shard_map(
        per_device,
        mesh=mesh,
        in_specs=(
            rows, P("dp", None, None), P(), P(), inward, inward, inward, P(), P(),
            outward, P(), P(), inward, outward, rows,
        ),
        out_specs=(
            rows, rows, P(), P(), inward, inward, inward, P(), P(),
            outward, P(), P(), inward, outward,
        ),
        check_vma=False,
    )
```

time: 2600 us -> 431 us (0.17)
  waiting for transfers between devices: 1820 us -> 161 us
  blocking collectives: 468 us -> 0 us
  matrix products: 170 us -> 0 us
  Pallas kernels: 0 us -> 107 us
  starting transfers between devices: 1.28 us -> 84.6 us
  other arithmetic: 64.8 us -> 28.3 us
    reduce_scatter x22 -> x0, waiting for transfers between devices: 1530 us -> none  [the longest x2 284 us: reduce_grads(): lax.psum_scatter(weight_part[3], ('dp', 'row'), scatter_dimension=0, tile...]
    all_gather x16 -> x0, blocking collectives: 387 us -> none  [the longest x2 94.7 us: fetch(): lax.all_gather(blocks[0], ('dp', 'row'), axis=0, tiled=True)]
    all_gather x8 -> x0, waiting for transfers between devices: 239 us -> none  [the longest x2 120 us: fetch(): lax.all_gather(blocks[3], ('dp', 'row'), axis=0, tiled=True)]
    ppermute x0 -> x68, waiting for transfers between devices: none -> 161 us  [the longest x28 113 us: swap_bit(): return lax.ppermute(x, axis, [(i, i ^ 1 << bit) for i in range(n)])]
    dot_general x46 -> x0, matrix products: 150 us -> none  [the longest x24 61.7 us: contract(): lax.dot_general(left_arr, right_arr, (((left_dim,), (right_dim,)), ((), (...]
    pallas_call x0 -> x12, Pallas kernels: none -> 107 us  [call(): pl.pallas_call(body, out_shape=[jax.ShapeDtypeStruct(s, d) for s, d in ou...]
    ppermute x0 -> x68, starting transfers between devices: none -> 84.6 us  [the longest x24 45.4 us: hop(): return lax.ppermute(x, 'row', pairs)]
    psum x2 -> x0, blocking collectives: 81.6 us -> none  [reduce_grads(): summed = lax.psum(gain_part, ('dp', 'row', 'col'))]
  transfers between devices with their start and end apart: 32 -> 68, of which waited for: 26 -> 29; matrix products, arithmetic and copies ran while one was open for 6% -> 7% of each run, Pallas kernels for 0% -> 8%
where the time goes in v1:
time: 431 us; the launch traced here: 425 us
  waiting for transfers between devices  161 us (37%)
  Pallas kernels  107 us (25%)
  starting transfers between devices  84.6 us (20%)
  local copies, waits for them, and re-layouts  42.3 us (10%)
  other arithmetic  28.3 us (7%)
    ppermute x28, waiting for transfers between devices, swap_bit(): return lax.ppermute(x, axis, [(i, i ^ 1 << bit) for i in range(n)])  113 us
    pallas_call x12, Pallas kernels, call(): pl.pallas_call(body, out_shape=[jax.ShapeDtypeStruct(s, d) for s, d in ou...  107 us
    ppermute x24, waiting for transfers between devices, hop(): return lax.ppermute(x, 'row', pairs)  46.7 us
    ppermute x24, starting transfers between devices, hop(): return lax.ppermute(x, 'row', pairs)  45.4 us
    ppermute x28, starting transfers between devices, swap_bit(): return lax.ppermute(x, axis, [(i, i ^ 1 << bit) for i in range(n)])  35.8 us
    unnamed x206, local copies, waits for them, and re-layouts  31.3 us
    convert_element_type x26, other arithmetic, add_low(): return (a.astype(F4) + b.astype(F4)).astype(BF)  9.13 us
  transfers between devices with their start and end apart: 68, of which 29 were waited for; matrix products, arithmetic and copies ran while one was open for 7% of the time, Pallas kernels for 8%

profile of v1, /device:TPU:0, one launch (start us, length us, event | category | flops | bytes accessed | tf_op | source)
XLA Modules:
  0.0 425.3 jit_solution(9584125533160732737)
XLA Ops:
  3.3 4.1 collective-permute-start.13
  12.9 3.9 collective-permute-done.1
  50.3 5.9 %collective-permute-done.19 = bf16[192,896]{1,0:T(8,128)(2,1)S(1)} collective-permute-done((bf16[192,896]{1,0:T(8,128)(2,1)S(1)}, bf16[192,896]{1,0:T(8,128)(2,1)S(1)}, u32[]{:S(2)}, u32[]{:S(2)}) %collective-permute-start.19) | collective-permute-done | bytes 344096 | tf_op jit(solution)/shard_map/ppermute | solution.py:39
  58.7 5.2 %collective-permute-done.16 = bf16[192,1024]{1,0:T(8,128)(2,1)S(1)} collective-permute-done((bf16[192,1024]{1,0:T(8,128)(2,1)S(1)}, bf16[192,1024]{1,0:T(8,128)(2,1)S(1)}, u32[]{:S(2)}, u32[]{:S(2)}) %collective-permute-start.16) | collective-permute-done | bytes 393248 | tf_op jit(solution)/shard_map/ppermute | solution.py:39
  68.3 10.4 %collective-permute-done.20 = bf16[2,192,896]{2,1,0:T(8,128)(2,1)S(1)} collective-permute-done((bf16[2,192,896]{2,1,0:T(8,128)(2,1)S(1)}, bf16[2,192,896]{2,1,0:T(8,128)(2,1)S(1)}, u32[]{:S(2)}, u32[]{:S(2)}) %collective-permute-start.20) | collective-permute-done | bytes 688160 | tf_op jit(solution)/shard_map/ppermute | solution.py:39
  79.4 13.4 %collective-permute-done.17 = bf16[2,192,1024]{2,1,0:T(8,128)(2,1)S(1)} collective-permute-done((bf16[2,192,1024]{2,1,0:T(8,128)(2,1)S(1)}, bf16[2,192,1024]{2,1,0:T(8,128)(2,1)S(1)}, u32[]{:S(2)}, u32[]{:S(2)}) %collective-permute-start.17) | collective-permute-done | bytes 786464 | tf_op jit(solution)/shard_map/ppermute | solution.py:39
  94.8 10.3 %collective-permute-done.11.refs_0_.refs_9_ = bf16[352,768]{1,0:T(8,128)(2,1)S(1)} collective-permute-done((bf16[352,768]{1,0:T(8,128)(2,1)S(1)}, bf16[352,768]{1,0:T(8,128)(2,1)S(1)}, u32[]{:S(2)}, u32[]{:S(2)}) %collective-permute-start.11) | collective-permute-done | bytes 540704 | tf_op jit(solution)/shard_map/ppermute | solution.py:35
  121.2 12.9 %shard_map.258 = (bf16[352,768]{1,0:T(8,128)(2,1)S(1)}, f32[352,128]{1,0:T(8,128)S(1)}) custom-call(bf16[352,768]{1,0:T(8,128)(2,1)S(1)} %get-tuple-element.82.refs_0_, s32[352,1]{1,0:T(8,128)S(1)} %copy.34.refs_1_.refs_6_, s32[1,1408]{1,0:T(1,128)S(1)} %concatenate.39.refs_2_, bf16[352,768]{1,0:T(8,128)(2,1)S(1)} %get-tuple-element.83.refs_3_.refs_1_, ...), custom_call_target="tpu_custom_call" | custom-call | flops 6090129408 | bytes 5593984 | tf_op jit(solution)/shard_map/pallas_call | solution.py:222
  134.2 11.3 %shard_map.259 = (f32[352,768]{1,0:T(8,128)S(1)}, bf16[352,768]{1,0:T(8,128)(2,1)S(1)}, bf16[352,3072]{1,0:T(8,128)(2,1)S(1)}, bf16[352,3072]{1,0:T(8,128)(2,1)S...) custom-call(bf16[352,768]{1,0:T(8,128)(2,1)S(1)} %get-tuple-element., ...), custom_call_target="tpu_custom_call" | custom-call | flops 3737124864 | bytes 18192384 | tf_op jit(solution)/shard_map/pallas_call | solution.py:222
  158.3 20.3 %shard_map.260 = (bf16[352,768]{1,0:T(8,128)(2,1)S(1)}, f32[352,768]{1,0:T(8,128)S(1)}, bf16[352,768]{1,0:T(8,128)(2,1)S(1)}, f32[352,128]{1,0:T(8,128)S(1)}, f3...) custom-call(f32[352,768]{1,0:T(8,128)S(1)} %copy-done.82, ...), custom_call_target="tpu_custom_call" | custom-call | flops 7474249728 | bytes 25895936 | tf_op jit(solution)/shard_map/pallas_call | solution.py:222
  179.8 10.3 %shard_map.264 = (bf16[352,768]{1,0:T(8,128)(2,1)S(1)}, bf16[352,768]{1,0:T(8,128)(2,1)S(1)}, f32[352,768]{1,0:T(8,128)S(1)}, bf16[352,768]{1,0:T(8,128)(2,1)S(1...) custom-call(bf16[352,768]{1,0:T(8,128)(2,1)S(1)} %copy-done.78, bf16[352,768]{1,0:T(8,128)(2,1)S(1)} %copy-done.68, ...), custom_call_target="tpu_custom_call" | custom-call | flops 4636803072 | bytes 10398464 | tf_op jit(solution)/shard_map/pallas_call | solution.py:222
  192.6 10.4 %shard_map.263 = (bf16[352,768]{1,0:T(8,128)(2,1)S(1)}, bf16[352,768]{1,0:T(8,128)(2,1)S(1)}, f32[352,768]{1,0:T(8,128)S(1)}, bf16[352,768]{1,0:T(8,128)(2,1)S(1...) custom-call(bf16[352,768]{1,0:T(8,128)(2,1)S(1)} %copy-done.78, bf16[352,768]{1,0:T(8,128)(2,1)S(1)} %copy-done.64, ...), custom_call_target="tpu_custom_call" | custom-call | flops 4636803072 | bytes 10398464 | tf_op jit(solution)/shard_map/pallas_call | solution.py:222
  205.4 10.3 %shard_map.262 = (bf16[352,768]{1,0:T(8,128)(2,1)S(1)}, bf16[352,768]{1,0:T(8,128)(2,1)S(1)}, f32[352,768]{1,0:T(8,128)S(1)}, bf16[352,768]{1,0:T(8,128)(2,1)S(1...) custom-call(bf16[352,768]{1,0:T(8,128)(2,1)S(1)} %copy-done.78, bf16[352,768]{1,0:T(8,128)(2,1)S(1)} %get-tuple-element.84.refs_4_.refs_1_, ...), custom_call_target="tpu_custom_call" | custom-call | flops 4636803072 | bytes 10398464 | tf_op jit(solution)/shard_map/pallas_call | solution.py:222
  216.8 10.5 %shard_map.261 = (bf16[352,768]{1,0:T(8,128)(2,1)S(1)}, bf16[352,768]{1,0:T(8,128)(2,1)S(1)}, f32[352,768]{1,0:T(8,128)S(1)}, f32[352,768]{1,0:T(8,128)S(1)}, f3...) custom-call(bf16[352,768]{1,0:T(8,128)(2,1)S(1)} %copy-done.78, bf16[352,768]{1,0:T(8,128)(2,1)S(1)} %copy-done.74, ...), custom_call_target="tpu_custom_call" | custom-call | flops 4636803072 | bytes 10939136 | tf_op jit(solution)/shard_map/pallas_call | solution.py:222
  228.9 10.8 %shard_map.265 = (f32[352,768]{1,0:T(8,128)S(1)}, f32[1,256]{1,0:T(1,128)S(1)}, f32[2,768]{1,0:T(2,128)S(1)}, bf16[768,640]{1,0:T(8,128)(2,1)S(1)}, bf16[768,640...) custom-call(f32[352,768]{1,0:T(8,128)S(1)} %get-tuple-element.98.refs_0_, ...), custom_call_target="tpu_custom_call" | custom-call | flops 4152360960 | bytes 20111360 | tf_op jit(solution)/shard_map/pallas_call | solution.py:222
  264.0 13.5 %collective-permute-done.40 = f32[28,128]{1,0:T(8,128)S(1)} collective-permute-done((f32[28,128]{1,0:T(8,128)S(1)}, f32[28,128]{1,0:T(8,128)S(1)}, u32[]{:S(2)}, u32[]{:S(2)}) %collective-permute-start.40) | collective-permute-done | bytes 14368 | tf_op jit(solution)/shard_map/ppermute | solution.py:39
  290.3 12.2 %collective-permute-done.33 = bf16[352,768]{1,0:T(8,128)(2,1)S(1)} collective-permute-done((bf16[352,768]{1,0:T(8,128)(2,1)S(1)}, bf16[352,768]{1,0:T(8,128)(2,1)S(1)}, u32[]{:S(2)}, u32[]{:S(2)}) %collective-permute-start.33) | collective-permute-done | bytes 540704 | tf_op jit(solution)/shard_map/ppermute | solution.py:35
  306.2 6.8 %collective-permute-done.45 = bf16[2,192,512]{2,1,0:T(8,128)(2,1)S(1)} collective-permute-done((bf16[2,192,512]{2,1,0:T(8,128)(2,1)S(1)}, bf16[2,192,512]{2,1,0:T(8,128)(2,1)S(1)}, u32[]{:S(2)}, u32[]{:S(2)}) %collective-permute-start.45) | collective-permute-done | bytes 393248 | tf_op jit(solution)/shard_map/ppermute | solution.py:39
  318.8 14.4 %collective-permute-done.46 = bf16[192,512]{1,0:T(8,128)(2,1)S(1)} collective-permute-done((bf16[192,512]{1,0:T(8,128)(2,1)S(1)}, bf16[192,512]{1,0:T(8,128)(2,1)S(1)}, u32[]{:S(2)}, u32[]{:S(2)}) %collective-permute-start.46) | collective-permute-done | bytes 196640 | tf_op jit(solution)/shard_map/ppermute | solution.py:39
  339.9 26.8 %collective-permute-done.43 = bf16[192,640]{1,0:T(8,128)(2,1)S(1)} collective-permute-done((bf16[192,640]{1,0:T(8,128)(2,1)S(1)}, bf16[192,640]{1,0:T(8,128)(2,1)S(1)}, u32[]{:S(2)}, u32[]{:S(2)}) %collective-permute-start.43) | collective-permute-done | bytes 245792 | tf_op jit(solution)/shard_map/ppermute | solution.py:39
  368.9 3.4 collective-permute-done.47
  386.4 4.3 collective-permute-done.64
  390.8 4.1 collective-permute-start.65
  408.2 3.7 collective-permute-done.56
  (468 shorter events, 183.4 us)
Async XLA Ops:
  12.8 27.5 %collective-permute-start = (bf16[2,176,768]{2,1,0:T(8,128)(2,1)S(1)}, bf16[2,176,768]{2,1,0:T(8,128)(2,1)S(1)}, u32[]{:S(2)}, u32[]{:S(2)}) collective-permute-start(bf16[2,176,768]{2,1,0:T(8,128)(2,1)S(1)} %select_bitcast_fusion.10), channel_id=1, source_target_pairs={{0,1},{1,0},{2,3},{3,2},{4,5},{5,4},{6,7},{7,6},{8,9},{9,8},{10,11... | collective-permute-start | bytes 1622024 | tf_op jit(solution)/shard_map/ppermute | solution.py:43
  41.8 37.0 %collective-permute-start.10 = (bf16[352,768]{1,0:T(8,128)(2,1)S(1)}, bf16[352,768]{1,0:T(8,128)(2,1)S(1)}, u32[]{:S(2)}, u32[]{:S(2)}) collective-permute-start(bf16[352,768]{1,0:T(8,128)(2,1)S(1)} %get-tuple-element.154.refs_0_.p.refs_9_.refs_2_), channel_id=1, source_target_pairs={{0,4},{4,6},{6,2},{2,0},{1,5},{5,7},{7,3},{3,1},{8,12},{12,14},{14... | collective-permute-start | bytes 1622024 | tf_op jit(solution)/shard_map/ppermute | solution.py:35
  56.2 37.5 %collective-permute-start.26 = (bf16[2,192,768]{2,1,0:T(8,128)(2,1)S(1)}, bf16[2,192,768]{2,1,0:T(8,128)(2,1)S(1)}, u32[]{:S(2)}, u32[]{:S(2)}) collective-permute-start(bf16[2,192,768]{2,1,0:T(8,128)(2,1)S(1)} %pad_maximum_fusion.11), channel_id=1, source_target_pairs={{0,16},{8,24},{16,0},{24,8},{1,17},{9,25},{17,1},{25,9},{2,18},{10... | collective-permute-start | bytes 1769480 | tf_op jit(solution)/shard_map/ppermute | solution.py:39
  64.1 28.8 %collective-permute-start.17 = (bf16[2,192,1024]{2,1,0:T(8,128)(2,1)S(1)}, bf16[2,192,1024]{2,1,0:T(8,128)(2,1)S(1)}, u32[]{:S(2)}, u32[]{:S(2)}) collective-permute-start(bf16[2,192,1024]{2,1,0:T(8,128)(2,1)S(1)} %pad_maximum_fusion.6), channel_id=1, source_target_pairs={{0,16},{8,24},{16,0},{24,8},{1,17},{9,25},{17,1},{25,9},{2,18},{10... | collective-permute-start | bytes 2359304 | tf_op jit(solution)/shard_map/ppermute | solution.py:39
  66.7 27.3 %collective-permute-start.29 = (bf16[2,192,768]{2,1,0:T(8,128)(2,1)S(1)}, bf16[2,192,768]{2,1,0:T(8,128)(2,1)S(1)}, u32[]{:S(2)}, u32[]{:S(2)}) collective-permute-start(bf16[2,192,768]{2,1,0:T(8,128)(2,1)S(1)} %pad_maximum_fusion.12), channel_id=1, source_target_pairs={{0,8},{8,0},{16,24},{24,16},{1,9},{9,1},{17,25},{25,17},{2,10},{10... | collective-permute-start | bytes 1769480 | tf_op jit(solution)/shard_map/ppermute | solution.py:39
  78.7 27.5 %collective-permute-start.9 = (bf16[768,512]{1,0:T(8,128)(2,1)S(1)}, bf16[768,512]{1,0:T(8,128)(2,1)S(1)}, u32[]{:S(2)}, u32[]{:S(2)}) collective-permute-start(bf16[768,512]{1,0:T(8,128)(2,1)S(1)} %bitcast.213), channel_id=1, source_target_pairs={{0,1},{1,0},{2,3},{3,2},{4,5},{5,4},{6,7},{7,6},{8,9},{9,8},{10,11... | collective-permute-start | bytes 2359304 | tf_op jit(solution)/shard_map/ppermute | solution.py:43
  78.9 27.4 %collective-permute-start.6 = (bf16[768,640]{1,0:T(8,128)(2,1)S(1)}, bf16[768,640]{1,0:T(8,128)(2,1)S(1)}, u32[]{:S(2)}, u32[]{:S(2)}) collective-permute-start(bf16[768,640]{1,0:T(8,128)(2,1)S(1)} %bitcast.203), channel_id=1, source_target_pairs={{0,1},{1,0},{2,3},{3,2},{4,5},{5,4},{6,7},{7,6},{8,9},{9,8},{10,11... | collective-permute-start | bytes 2949128 | tf_op jit(solution)/shard_map/ppermute | solution.py:43
  93.7 40.5 %collective-permute-start.18 = (bf16[768,1024]{1,0:T(8,128)(2,1)S(1)}, bf16[768,1024]{1,0:T(8,128)(2,1)S(1)}, u32[]{:S(2)}, u32[]{:S(2)}) collective-permute-start(bf16[768,1024]{1,0:T(8,128)(2,1)S(1)} %bitcast.222), channel_id=1, source_target_pairs={{0,1},{1,0},{2,3},{3,2},{4,5},{5,4},{6,7},{7,6},{8,9},{9,8},{10,11... | collective-permute-start | bytes 4718600 | tf_op jit(solution)/shard_map/ppermute | solution.py:43
  94.0 40.1 %collective-permute-start.21 = (bf16[768,896]{1,0:T(8,128)(2,1)S(1)}, bf16[768,896]{1,0:T(8,128)(2,1)S(1)}, u32[]{:S(2)}, u32[]{:S(2)}) collective-permute-start(bf16[768,896]{1,0:T(8,128)(2,1)S(1)} %bitcast.225), channel_id=1, source_target_pairs={{0,1},{1,0},{2,3},{3,2},{4,5},{5,4},{6,7},{7,6},{8,9},{9,8},{10,11... | collective-permute-start | bytes 4128776 | tf_op jit(solution)/shard_map/ppermute | solution.py:43
  106.1 48.1 %collective-permute-start.30 = (bf16[768,768]{1,0:T(8,128)(2,1)S(1)}, bf16[768,768]{1,0:T(8,128)(2,1)S(1)}, u32[]{:S(2)}, u32[]{:S(2)}) collective-permute-start(bf16[768,768]{1,0:T(8,128)(2,1)S(1)} %bitcast.228), channel_id=1, source_target_pairs={{0,1},{1,0},{2,3},{3,2},{4,5},{5,4},{6,7},{7,6},{8,9},{9,8},{10,11... | collective-permute-start | bytes 3538952 | tf_op jit(solution)/shard_map/ppermute | solution.py:43
  106.2 48.0 %collective-permute-start.27 = (bf16[768,768]{1,0:T(8,128)(2,1)S(1)}, bf16[768,768]{1,0:T(8,128)(2,1)S(1)}, u32[]{:S(2)}, u32[]{:S(2)}) collective-permute-start(bf16[768,768]{1,0:T(8,128)(2,1)S(1)} %bitcast.230), channel_id=1, source_target_pairs={{0,1},{1,0},{2,3},{3,2},{4,5},{5,4},{6,7},{7,6},{8,9},{9,8},{10,11... | collective-permute-start | bytes 3538952 | tf_op jit(solution)/shard_map/ppermute | solution.py:43
  260.5 43.3 %collective-permute-start.59 = (bf16[768,768]{1,0:T(8,128)(2,1)}, bf16[768,768]{1,0:T(8,128)(2,1)}, u32[]{:S(2)}, u32[]{:S(2)}) collective-permute-start(bf16[768,768]{1,0:T(8,128)(2,1)} %copy-done.51), channel_id=1, source_target_pairs={{0,1},{1,0},{2,3},{3,2},{4,5},{5,4},{6,7},{7,6},{8,9},{9,8},{10,11... | collective-permute-start | bytes 3538952 | tf_op jit(solution)/shard_map/ppermute | solution.py:43
  260.5 54.0 %collective-permute-start.62 = (bf16[768,768]{1,0:T(8,128)(2,1)}, bf16[768,768]{1,0:T(8,128)(2,1)}, u32[]{:S(2)}, u32[]{:S(2)}) collective-permute-start(bf16[768,768]{1,0:T(8,128)(2,1)} %copy-done.50), channel_id=1, source_target_pairs={{0,1},{1,0},{2,3},{3,2},{4,5},{5,4},{6,7},{7,6},{8,9},{9,8},{10,11... | collective-permute-start | bytes 3538952 | tf_op jit(solution)/shard_map/ppermute | solution.py:43
  261.0 26.6 %collective-permute-start.44 = (bf16[768,512]{1,0:T(8,128)(2,1)}, bf16[768,512]{1,0:T(8,128)(2,1)}, u32[]{:S(2)}, u32[]{:S(2)}) collective-permute-start(bf16[768,512]{1,0:T(8,128)(2,1)} %copy-done.59), channel_id=1, source_target_pairs={{0,1},{1,0},{2,3},{3,2},{4,5},{5,4},{6,7},{7,6},{8,9},{9,8},{10,11... | collective-permute-start | bytes 2359304 | tf_op jit(solution)/shard_map/ppermute | solution.py:43
  261.0 25.3 %collective-permute-start.32 = (bf16[352,768]{1,0:T(8,128)(2,1)}, bf16[352,768]{1,0:T(8,128)(2,1)}, u32[]{:S(2)}, u32[]{:S(2)}) collective-permute-start(bf16[352,768]{1,0:T(8,128)(2,1)} %copy-done.60), channel_id=1, source_target_pairs={{0,4},{4,6},{6,2},{2,0},{1,5},{5,7},{7,3},{3,1},{8,12},{12,14},{14... | collective-permute-start | bytes 1622024 | tf_op jit(solution)/shard_map/ppermute | solution.py:35
  286.3 49.2 %collective-permute-start.50 = (bf16[768,1024]{1,0:T(8,128)(2,1)S(1)}, bf16[768,1024]{1,0:T(8,128)(2,1)S(1)}, u32[]{:S(2)}, u32[]{:S(2)}) collective-permute-start(bf16[768,1024]{1,0:T(8,128)(2,1)S(1)} %copy-done.101), channel_id=1, source_target_pairs={{0,1},{1,0},{2,3},{3,2},{4,5},{5,4},{6,7},{7,6},{8,9},{9,8},{10,11... | collective-permute-start | bytes 4718600 | tf_op jit(solution)/shard_map/ppermute | solution.py:43
  289.6 28.1 %collective-permute-start.53 = (bf16[768,896]{1,0:T(8,128)(2,1)S(1)}, bf16[768,896]{1,0:T(8,128)(2,1)S(1)}, u32[]{:S(2)}, u32[]{:S(2)}) collective-permute-start(bf16[768,896]{1,0:T(8,128)(2,1)S(1)} %copy-done.49), channel_id=1, source_target_pairs={{0,1},{1,0},{2,3},{3,2},{4,5},{5,4},{6,7},{7,6},{8,9},{9,8},{10,11... | collective-permute-start | bytes 4128776 | tf_op jit(solution)/shard_map/ppermute | solution.py:43
  303.8 30.3 %collective-permute-start.42 = (bf16[2,192,640]{2,1,0:T(8,128)(2,1)S(1)}, bf16[2,192,640]{2,1,0:T(8,128)(2,1)S(1)}, u32[]{:S(2)}, u32[]{:S(2)}) collective-permute-start(bf16[2,192,640]{2,1,0:T(8,128)(2,1)S(1)} %dynamic-slice_bitcast_fusion.4), channel_id=1, source_target_pairs={{0,8},{8,0},{16,24},{24,16},{1,9},{9,1},{17,25},{25,17},{2,10},{10... | collective-permute-start | bytes 1474568 | tf_op jit(solution)/shard_map/ppermute | solution.py:39
  314.5 52.3 %collective-permute-start.60 = (bf16[2,192,768]{2,1,0:T(8,128)(2,1)S(1)}, bf16[2,192,768]{2,1,0:T(8,128)(2,1)S(1)}, u32[]{:S(2)}, u32[]{:S(2)}) collective-permute-start(bf16[2,192,768]{2,1,0:T(8,128)(2,1)S(1)} %dynamic-slice_bitcast_fusion.3), channel_id=1, source_target_pairs={{0,8},{8,0},{16,24},{24,16},{1,9},{9,1},{17,25},{25,17},{2,10},{10... | collective-permute-start | bytes 1769480 | tf_op jit(solution)/shard_map/ppermute | solution.py:39
  333.1 39.8 %collective-permute-start.63 = (bf16[2,192,768]{2,1,0:T(8,128)(2,1)S(1)}, bf16[2,192,768]{2,1,0:T(8,128)(2,1)S(1)}, u32[]{:S(2)}, u32[]{:S(2)}) collective-permute-start(bf16[2,192,768]{2,1,0:T(8,128)(2,1)S(1)} %dynamic-slice_bitcast_fusion.2), channel_id=1, source_target_pairs={{0,16},{8,24},{16,0},{24,8},{1,17},{9,25},{17,1},{25,9},{2,18},{10... | collective-permute-start | bytes 1769480 | tf_op jit(solution)/shard_map/ppermute | solution.py:39
  334.1 60.8 %collective-permute-start.54 = (bf16[2,192,896]{2,1,0:T(8,128)(2,1)S(1)}, bf16[2,192,896]{2,1,0:T(8,128)(2,1)S(1)}, u32[]{:S(2)}, u32[]{:S(2)}) collective-permute-start(bf16[2,192,896]{2,1,0:T(8,128)(2,1)S(1)} %dynamic-slice_bitcast_fusion.1), channel_id=1, source_target_pairs={{0,16},{8,24},{16,0},{24,8},{1,17},{9,25},{17,1},{25,9},{2,18},{10... | collective-permute-start | bytes 2064392 | tf_op jit(solution)/shard_map/ppermute | solution.py:39
  335.5 31.1 %collective-permute-start.43 = (bf16[192,640]{1,0:T(8,128)(2,1)S(1)}, bf16[192,640]{1,0:T(8,128)(2,1)S(1)}, u32[]{:S(2)}, u32[]{:S(2)}) collective-permute-start(bf16[192,640]{1,0:T(8,128)(2,1)S(1)} %dynamic-slice_bitcast_fusion.10), channel_id=1, source_target_pairs={{0,16},{8,24},{16,0},{24,8},{1,17},{9,25},{17,1},{25,9},{2,18},{10... | collective-permute-start | bytes 737288 | tf_op jit(solution)/shard_map/ppermute | solution.py:39
  337.3 59.6 %collective-permute-start.51 = (bf16[2,192,1024]{2,1,0:T(8,128)(2,1)S(1)}, bf16[2,192,1024]{2,1,0:T(8,128)(2,1)S(1)}, u32[]{:S(2)}, u32[]{:S(2)}) collective-permute-start(bf16[2,192,1024]{2,1,0:T(8,128)(2,1)S(1)} %dynamic-slice_bitcast_fusion), channel_id=1, source_target_pairs={{0,8},{8,0},{16,24},{24,16},{1,9},{9,1},{17,25},{25,17},{2,10},{10... | collective-permute-start | bytes 2359304 | tf_op jit(solution)/shard_map/ppermute | solution.py:39
  366.6 31.7 %collective-permute-start.35 = (f32[176,768]{1,0:T(8,128)S(1)}, f32[176,768]{1,0:T(8,128)S(1)}, u32[]{:S(2)}, u32[]{:S(2)}) collective-permute-start(f32[176,768]{1,0:T(8,128)S(1)} %slice_select_fusion), channel_id=1, source_target_pairs={{0,1},{1,0},{2,3},{3,2},{4,5},{5,4},{6,7},{7,6},{8,9},{9,8},{10,11... | collective-permute-start | bytes 1622024 | tf_op jit(solution)/shard_map/ppermute | solution.py:43
  (146 other events, 1479.7 us)
